TPU v7x, 256 devices: a whole 4x4x8 slice. The times are simulated.
256 devices in a mesh: ctx: 64 (over z, x_hi, y), tp: 4 (over x_lo, core).
Axes of the slice: x: 4 (x_hi: 2, x_lo: 2; x = x_hi * 2 + x_lo), y: 4, z: 8, core: 2. Of those that a mesh axis runs over, the one named last changes fastest.
Arguments:
- hit_features: bfloat16 [24576, 1024], P('ctx', 'tp'), may hold values from -6 to 6
- segment: int32 [24576], P('ctx'), may hold values from 0 to 31, never falling along the last dimension, each value on 1 to 1537 neighbouring positions
- norm1_gain: float32 [1024], replicated, may hold values from 0.1 to 1.9
- w_qkv: bfloat16 [3, 1024, 1024], P(None, None, 'tp'), may hold values from -2 to 2
- w_out: bfloat16 [1024, 1024], P('tp'), may hold values from -0.1875 to 0.1875
- norm2_gain: float32 [1024], replicated, may hold values from 0.1 to 1.9
- w_up: bfloat16 [1024, 4096], P(None, 'tp'), may hold values from -0.1875 to 0.1875
- w_down: bfloat16 [4096, 1024], P('tp'), may hold values from -0.09375 to 0.09375
Outputs:
- layer_out: bfloat16 [24576, 1024], P('ctx', 'tp')
Inputs may be any that keep to these rules, and one draw needn't show every extreme that they name: `segment`: never falls from one hit to the next; every event number below 32 appears; each event holds 1 to 1537 consecutive hits and some event holds exactly 1537.
All inputs are finite; a program needn't handle non-finite values.
Results may differ from a plain program's by a relative error of at most 0.014.
Values may be sent and summed in bfloat16 or wider, within the bound.
No kernel may reach another device: no remote copies, remote signals or barrier semaphores. Data moves between devices by JAX's collectives and lax.ppermute only.
A program may use at most 128 MiB of HBM per device.

v0:
```python
import jax
import jax.numpy as jnp
from jax import lax
from jax.sharding import PartitionSpec as P

HEAD_DIM = 64
REACH = 4
epsilon = 1e-05
neg_fill = -1e30


def shifted(block, axis, distance):
    devices = range(lax.axis_size(axis))
    route = [(i - distance, i) for i in devices if i - distance in devices]
    return lax.ppermute(block, axis, route)


def rms_scale(features, gain):
    mean_square = jnp.mean(features * features, axis=-1, keepdims=True)
    return features * lax.rsqrt(mean_square + epsilon) * gain


def absorb(carry_state, query_heads, event_tag, key_rows, value_rows, key_tag):
    row_top, row_total, weighted = carry_state
    head_count = query_heads.shape[1]
    key_heads = key_rows.reshape(key_rows.shape[0], head_count, HEAD_DIM)
    value_heads = value_rows.reshape(value_rows.shape[0], head_count, HEAD_DIM)
    scores = jnp.einsum("qhd,khd->hqk", query_heads, key_heads, preferred_element_type=jnp.float32)
    matches = (event_tag[:, None] == key_tag[None, :])[None]
    masked = jnp.where(matches, scores, neg_fill)
    new_top = jnp.maximum(row_top, jnp.max(masked, axis=-1, keepdims=True))
    powered = jnp.where(matches, jnp.exp(masked - new_top), 0.0)
    rescale = jnp.exp(row_top - new_top)
    row_total = row_total * rescale + jnp.sum(powered, axis=-1, keepdims=True)
    weighted = weighted * rescale + jnp.einsum(
        "hqk,khd->hqd",
        powered.astype(jnp.bfloat16),
        value_heads,
        preferred_element_type=jnp.float32,
    )
    return (new_top, row_total, weighted)


def shards(hit_features, segment, norm1_gain, w_qkv, w_out, norm2_gain, w_up, w_down):
    features = lax.all_gather(hit_features, "tp", axis=1, tiled=True).astype(jnp.float32)
    normed = rms_scale(features, norm1_gain).astype(jnp.bfloat16)
    projected = jnp.einsum("td,cde->cte", normed, w_qkv, preferred_element_type=jnp.float32)
    queries = (projected[0] * HEAD_DIM ** (-0.5)).astype(jnp.bfloat16)
    key_rows = projected[1].astype(jnp.bfloat16)
    value_rows = projected[2].astype(jnp.bfloat16)
    hit_count = hit_features.shape[0]
    head_count = w_qkv.shape[2] // HEAD_DIM
    query_heads = queries.reshape(hit_count, head_count, HEAD_DIM)
    event_tag = segment + 1
    carry_state = (
        jnp.full((head_count, hit_count, 1), neg_fill, jnp.float32),
        jnp.zeros((head_count, hit_count, 1), jnp.float32),
        jnp.zeros((head_count, hit_count, HEAD_DIM), jnp.float32),
    )
    carry_state = absorb(carry_state, query_heads, event_tag, key_rows, value_rows, event_tag)
    lower = (key_rows, value_rows, event_tag)
    upper = (key_rows, value_rows, event_tag)
    for offset in range(REACH):
        lower = shifted((lower[0], lower[1], lower[2]), "ctx", 1)
        upper = shifted((upper[0], upper[1], upper[2]), "ctx", -1)
        carry_state = absorb(carry_state, query_heads, event_tag, lower[0], lower[1], lower[2])
        carry_state = absorb(carry_state, query_heads, event_tag, upper[0], upper[1], upper[2])
    row_top, row_total, weighted = carry_state
    mixed_heads = (
        jnp.transpose(weighted / row_total, (1, 0, 2))
        .reshape(hit_count, head_count * HEAD_DIM)
        .astype(jnp.bfloat16)
    )
    attn_part = jnp.dot(mixed_heads, w_out, preferred_element_type=jnp.float32)
    residual = features + lax.psum(attn_part.astype(jnp.bfloat16), "tp").astype(jnp.float32)
    normed_second = rms_scale(residual, norm2_gain).astype(jnp.bfloat16)
    hidden = jax.nn.gelu(
        jnp.dot(normed_second, w_up, preferred_element_type=jnp.float32), approximate=False
    ).astype(jnp.bfloat16)
    ffn_part = jnp.dot(hidden, w_down, preferred_element_type=jnp.float32)
    ffn_share = lax.psum_scatter(
        ffn_part.astype(jnp.bfloat16), "tp", scatter_dimension=1, tiled=True
    ).astype(jnp.float32)
    share_width = ffn_share.shape[1]
    residual_share = lax.dynamic_slice_in_dim(
        residual, lax.axis_index("tp") * share_width, share_width, 1
    )
    return (residual_share + ffn_share).astype(jnp.bfloat16)


def solution(mesh):
    return jax.shard_map(
        shards,
        mesh=mesh,
        in_specs=(
            P("ctx", "tp"),
            P("ctx"),
            P(),
            P(None, None, "tp"),
            P("tp", None),
            P(),
            P(None, "tp"),
            P("tp", None),
        ),
        out_specs=P("ctx", "tp"),
        check_vma=False,
    )
```

profile of v0, /device:TPU:1, one launch (start us, length us, event | category | flops | bytes accessed | tf_op | source)
XLA Modules:
  0.0 243.1 jit_solution(5882714588632567019)
XLA Ops:
  6.5 0.8 broadcast_add_fusion
  7.4 4.0 %collective-permute-start = (s32[384]{0:T(512)S(1)}, s32[384]{0:T(512)S(1)}, u32[]{:S(2)}, u32[]{:S(2)}) collective-permute-start(s32[384]{0:T(512)S(1)} %broadcast_add_fusion), channel_id=1, source_target_pairs={{0,4},{4,8},{8,12},{12,16},{16,20},{20,24},{24,28},{28,32},{32,36}... | collective-permute-start | bytes 4616 | tf_op jit(solution)/shard_map/ppermute | solution.py:15
  11.4 1.3 collective-permute-start.3
  12.7 9.6 %all_gather.3 = bf16[384,1024]{1,0:T(8,128)(2,1)S(1)} all-gather(bf16[384,256]{1,0:T(8,128)(2,1)} %param.8), channel_id=1, replica_groups=mesh['ctx'=64,'tp'=4] {'tp'}, dimensions={1}, use_global_device_ids=true | all-gather | bytes 983040 | tf_op jit(solution)/shard_map/all_gather | solution.py:45
  22.5 4.3 %collective-permute-start.6 = (s32[384]{0:T(512)S(1)}, s32[384]{0:T(512)S(1)}, u32[]{:S(2)}, u32[]{:S(2)}) collective-permute-start(s32[384]{0:T(512)S(1)} %collective-permute-done), channel_id=1, source_target_pairs={{0,4},{4,8},{8,12},{12,16},{16,20},{20,24},{24,28},{28,32},{32,36}... | collective-permute-start | bytes 4616 | tf_op jit(solution)/shard_map/ppermute | solution.py:15
  26.8 1.3 collective-permute-start.9
  28.1 2.5 %convolution_bitcast_fusion = f32[3,384,256]{1,2,0:T(8,128)S(1)} fusion(bf16[3,1024,256]{2,1,0:T(8,128)(2,1)} %param.11, bf16[384,1024]{1,0:T(8,128)(2,1)S(1)} %all_gather.3, f32[1024]{0:T(1024)} %param.10, f32[384]{0:T(512)S(1)} %add_rsqrt_fusion.1), kind=kOutput, calls=%fused_computation.64 | convolution fusion | flops 605552640 | bytes 3544576 | tf_op jit(solution)/shard_map/td,cde->cte/dot_general | solution.py:47
  30.7 4.0 %collective-permute-start.12 = (s32[384]{0:T(512)S(1)}, s32[384]{0:T(512)S(1)}, u32[]{:S(2)}, u32[]{:S(2)}) collective-permute-start(s32[384]{0:T(512)S(1)} %collective-permute-done.6), channel_id=1, source_target_pairs={{0,4},{4,8},{8,12},{12,16},{16,20},{20,24},{24,28},{28,32},{32,36}... | collective-permute-start | bytes 4616 | tf_op jit(solution)/shard_map/ppermute | solution.py:15
  34.7 1.3 collective-permute-start.15
  36.0 4.0 %collective-permute-start.1 = (bf16[384,256]{0,1:T(8,128)(2,1)S(1)}, bf16[384,256]{0,1:T(8,128)(2,1)S(1)}, u32[]{:S(2)}, u32[]{:S(2)}) collective-permute-start(bf16[384,256]{0,1:T(8,128)(2,1)S(1)} %bitcast.263), channel_id=1, source_target_pairs={{0,4},{4,8},{8,12},{12,16},{16,20},{20,24},{24,28},{28,32},{32,36}... | collective-permute-start | bytes 589832 | tf_op jit(solution)/shard_map/ppermute | solution.py:15
  40.0 1.3 collective-permute-start.4
  41.3 1.3 collective-permute-start.5
  42.6 8.3 %collective-permute-start.18 = (s32[384]{0:T(512)S(1)}, s32[384]{0:T(512)S(1)}, u32[]{:S(2)}, u32[]{:S(2)}) collective-permute-start(s32[384]{0:T(512)S(1)} %collective-permute-done.12), channel_id=1, source_target_pairs={{0,4},{4,8},{8,12},{12,16},{16,20},{20,24},{24,28},{28,32},{32,36}... | collective-permute-start | bytes 4616 | tf_op jit(solution)/shard_map/ppermute | solution.py:15
  50.9 1.3 collective-permute-start.21
  52.3 7.6 %collective-permute-start.2 = (bf16[384,256]{0,1:T(8,128)(2,1)S(1)}, bf16[384,256]{0,1:T(8,128)(2,1)S(1)}, u32[]{:S(2)}, u32[]{:S(2)}) collective-permute-start(bf16[384,256]{0,1:T(8,128)(2,1)S(1)} %bitcast.275), channel_id=1, source_target_pairs={{0,4},{4,8},{8,12},{12,16},{16,20},{20,24},{24,28},{28,32},{32,36}... | collective-permute-start | bytes 589832 | tf_op jit(solution)/shard_map/ppermute | solution.py:15
  59.9 1.0 broadcast_compare_fusion.8
  61.5 7.0 %collective-permute-start.7 = (bf16[384,256]{0,1:T(8,128)(2,1)S(1)}, bf16[384,256]{0,1:T(8,128)(2,1)S(1)}, u32[]{:S(2)}, u32[]{:S(2)}) collective-permute-start(bf16[384,256]{0,1:T(8,128)(2,1)S(1)} %collective-permute-done.1), channel_id=1, source_target_pairs={{0,4},{4,8},{8,12},{12,16},{16,20},{20,24},{24,28},{28,32},{32,36}... | collective-permute-start | bytes 589832 | tf_op jit(solution)/shard_map/ppermute | solution.py:15
  68.5 1.3 collective-permute-start.10
  69.8 1.3 collective-permute-start.11
  71.7 8.2 %collective-permute-start.8 = (bf16[384,256]{0,1:T(8,128)(2,1)S(1)}, bf16[384,256]{0,1:T(8,128)(2,1)S(1)}, u32[]{:S(2)}, u32[]{:S(2)}) collective-permute-start(bf16[384,256]{0,1:T(8,128)(2,1)S(1)} %collective-permute-done.2), channel_id=1, source_target_pairs={{0,4},{4,8},{8,12},{12,16},{16,20},{20,24},{24,28},{28,32},{32,36}... | collective-permute-start | bytes 589832 | tf_op jit(solution)/shard_map/ppermute | solution.py:15
  79.9 0.6 select_reduce_fusion.6
  80.6 7.0 %collective-permute-start.13 = (bf16[384,256]{0,1:T(8,128)(2,1)S(1)}, bf16[384,256]{0,1:T(8,128)(2,1)S(1)}, u32[]{:S(2)}, u32[]{:S(2)}) collective-permute-start(bf16[384,256]{0,1:T(8,128)(2,1)S(1)} %collective-permute-done.7), channel_id=1, source_target_pairs={{0,4},{4,8},{8,12},{12,16},{16,20},{20,24},{24,28},{28,32},{32,36}... | collective-permute-start | bytes 589832 | tf_op jit(solution)/shard_map/ppermute | solution.py:15
  87.5 1.3 collective-permute-start.16
  89.4 1.3 collective-permute-start.17
  91.3 4.6 %collective-permute-start.14 = (bf16[384,256]{0,1:T(8,128)(2,1)S(1)}, bf16[384,256]{0,1:T(8,128)(2,1)S(1)}, u32[]{:S(2)}, u32[]{:S(2)}) collective-permute-start(bf16[384,256]{0,1:T(8,128)(2,1)S(1)} %collective-permute-done.8), channel_id=1, source_target_pairs={{0,4},{4,8},{8,12},{12,16},{16,20},{20,24},{24,28},{28,32},{32,36}... | collective-permute-start | bytes 589832 | tf_op jit(solution)/shard_map/ppermute | solution.py:15
  96.0 7.0 %collective-permute-start.19 = (bf16[384,256]{0,1:T(8,128)(2,1)S(1)}, bf16[384,256]{0,1:T(8,128)(2,1)S(1)}, u32[]{:S(2)}, u32[]{:S(2)}) collective-permute-start(bf16[384,256]{0,1:T(8,128)(2,1)S(1)} %collective-permute-done.13), channel_id=1, source_target_pairs={{0,4},{4,8},{8,12},{12,16},{16,20},{20,24},{24,28},{28,32},{32,36}... | collective-permute-start | bytes 589832 | tf_op jit(solution)/shard_map/ppermute | solution.py:15
  103.0 1.3 collective-permute-start.22
  104.3 1.3 collective-permute-start.23
  106.2 4.8 %collective-permute-start.20 = (bf16[384,256]{0,1:T(8,128)(2,1)S(1)}, bf16[384,256]{0,1:T(8,128)(2,1)S(1)}, u32[]{:S(2)}, u32[]{:S(2)}) collective-permute-start(bf16[384,256]{0,1:T(8,128)(2,1)S(1)} %collective-permute-done.14), channel_id=1, source_target_pairs={{0,4},{4,8},{8,12},{12,16},{16,20},{20,24},{24,28},{28,32},{32,36}... | collective-permute-start | bytes 589832 | tf_op jit(solution)/shard_map/ppermute | solution.py:15
  112.8 0.7 convolution_bitcast_fusion.7
  113.5 1.0 fusion.4
  114.5 0.7 convolution_bitcast_fusion.5
  115.2 1.0 fusion.8
  116.2 0.7 convolution_bitcast_fusion.3
  116.9 1.0 fusion.12
  118.4 1.0 fusion
  119.5 0.7 fusion.36
  120.2 0.7 fusion.39
  120.9 0.7 fusion.42
  121.6 0.7 fusion.45
  122.3 0.7 convolution_bitcast_fusion.1
  123.0 0.9 fusion.85
  124.0 1.3 convolution_convert_fusion
  125.4 75.8 %all-reduce.2.cloned.1.call-done = bf16[384,1024]{1,0:T(8,128)(2,1)} async-done(((bf16[384,1024]{1,0:T(8,128)(2,1)}), bf16[384,1024]{1,0:T(8,128)(2,1)}) %all-reduce.2.cloned.1.call-update) | async-done | bytes 786448 | tf_op jit(solution)/shard_map/psum | solution.py:75
  201.2 2.5 %convert_add_fusion = (f32[384,1024]{1,0:T(8,128)}, f32[384]{0:T(512)S(1)}) fusion(bf16[384,1024]{1,0:T(8,128)(2,1)S(1)} %all_gather.3, bf16[384,1024]{1,0:T(8,128)(2,1)} %all-reduce.2.cloned.1.call-done), kind=kLoop, calls=%fused_computation.1 | loop fusion | flops 1965696 | bytes 3147264 | tf_op jit(solution)/shard_map/add | solution.py:75
  203.8 7.6 %convolution_convert_fusion.1 = bf16[384,1024]{1,0:T(8,128)(2,1)} fusion(bf16[1024,1024]{1,0:T(8,128)(2,1)S(1)} %copy-done, bf16[1024,1024]{1,0:T(8,128)(2,1)} %param.14, f32[1024]{0:T(1024)S(1)} %copy-done.2, f32[384]{0:T(512)S(1)} %add_rsqrt_fusion, bf16[384,1024]{1,0:T(8,128)(2,1)S(1)} %all_gather.3, bf16[384,1024]{1,0:T(8,128)(2,1)} %all-reduce.2.cloned.1.call-done), kind=kOutput, calls=%fused_computation.65 | convolution fusion | flops 1638924288 | bytes 6559232 | tf_op jit(solution)/shard_map/dot_general | solution.py:80
  211.4 23.1 %reduce-scatter.2.cloned.1.call-done = bf16[384,256]{1,0:T(8,128)(2,1)} async-done(((bf16[384,1024]{1,0:T(8,128)(2,1)}), bf16[384,256]{1,0:T(8,128)(2,1)}) %reduce-scatter.2.cloned.1.call-update) | async-done | bytes 196624 | tf_op jit(solution)/shard_map/reduce_scatter | solution.py:81
  234.5 1.8 add_convert_fusion
  (51 shorter events, 5.9 us)
Async XLA Ops:
  6.5 197.2 %copy-start = (bf16[1024,1024]{1,0:T(8,128)(2,1)S(1)}, bf16[1024,1024]{1,0:T(8,128)(2,1)}, u32[]{:S(2)}) copy-start(bf16[1024,1024]{1,0:T(8,128)(2,1)} %param.15) | copy-start | bytes 6291460
  6.5 194.7 %all-reduce.2.cloned.1.call-start = ((), (), s32[]{:S(2)}) async-start(), calls=%async_computation.1 | async-start | bytes 1572864 | tf_op jit(solution)/shard_map/psum | solution.py:75
  7.4 15.2 %collective-permute-start = (s32[384]{0:T(512)S(1)}, s32[384]{0:T(512)S(1)}, u32[]{:S(2)}, u32[]{:S(2)}) collective-permute-start(s32[384]{0:T(512)S(1)} %broadcast_add_fusion), channel_id=1, source_target_pairs={{0,4},{4,8},{8,12},{12,16},{16,20},{20,24},{24,28},{28,32},{32,36}... | collective-permute-start | bytes 4616 | tf_op jit(solution)/shard_map/ppermute | solution.py:15
  11.4 15.4 %collective-permute-start.3 = (s32[384]{0:T(512)S(1)}, s32[384]{0:T(512)S(1)}, u32[]{:S(2)}, u32[]{:S(2)}) collective-permute-start(s32[384]{0:T(512)S(1)} %broadcast_add_fusion), channel_id=1, source_target_pairs={{4,0},{8,4},{12,8},{16,12},{20,16},{24,20},{28,24},{32,28},{36,32}... | collective-permute-start | bytes 4616 | tf_op jit(solution)/shard_map/ppermute | solution.py:15
  22.5 8.1 %collective-permute-start.6 = (s32[384]{0:T(512)S(1)}, s32[384]{0:T(512)S(1)}, u32[]{:S(2)}, u32[]{:S(2)}) collective-permute-start(s32[384]{0:T(512)S(1)} %collective-permute-done), channel_id=1, source_target_pairs={{0,4},{4,8},{8,12},{12,16},{16,20},{20,24},{24,28},{28,32},{32,36}... | collective-permute-start | bytes 4616 | tf_op jit(solution)/shard_map/ppermute | solution.py:15
  26.8 7.8 %collective-permute-start.9 = (s32[384]{0:T(512)S(1)}, s32[384]{0:T(512)S(1)}, u32[]{:S(2)}, u32[]{:S(2)}) collective-permute-start(s32[384]{0:T(512)S(1)} %collective-permute-done.3), channel_id=1, source_target_pairs={{4,0},{8,4},{12,8},{16,12},{20,16},{24,20},{28,24},{32,28},{36,32}... | collective-permute-start | bytes 4616 | tf_op jit(solution)/shard_map/ppermute | solution.py:15
  30.7 12.0 %collective-permute-start.12 = (s32[384]{0:T(512)S(1)}, s32[384]{0:T(512)S(1)}, u32[]{:S(2)}, u32[]{:S(2)}) collective-permute-start(s32[384]{0:T(512)S(1)} %collective-permute-done.6), channel_id=1, source_target_pairs={{0,4},{4,8},{8,12},{12,16},{16,20},{20,24},{24,28},{28,32},{32,36}... | collective-permute-start | bytes 4616 | tf_op jit(solution)/shard_map/ppermute | solution.py:15
  34.7 16.3 %collective-permute-start.15 = (s32[384]{0:T(512)S(1)}, s32[384]{0:T(512)S(1)}, u32[]{:S(2)}, u32[]{:S(2)}) collective-permute-start(s32[384]{0:T(512)S(1)} %collective-permute-done.9), channel_id=1, source_target_pairs={{4,0},{8,4},{12,8},{16,12},{20,16},{24,20},{28,24},{32,28},{36,32}... | collective-permute-start | bytes 4616 | tf_op jit(solution)/shard_map/ppermute | solution.py:15
  36.0 25.5 %collective-permute-start.1 = (bf16[384,256]{0,1:T(8,128)(2,1)S(1)}, bf16[384,256]{0,1:T(8,128)(2,1)S(1)}, u32[]{:S(2)}, u32[]{:S(2)}) collective-permute-start(bf16[384,256]{0,1:T(8,128)(2,1)S(1)} %bitcast.263), channel_id=1, source_target_pairs={{0,4},{4,8},{8,12},{12,16},{16,20},{20,24},{24,28},{28,32},{32,36}... | collective-permute-start | bytes 589832 | tf_op jit(solution)/shard_map/ppermute | solution.py:15
  40.0 28.5 %collective-permute-start.4 = (bf16[384,256]{0,1:T(8,128)(2,1)S(1)}, bf16[384,256]{0,1:T(8,128)(2,1)S(1)}, u32[]{:S(2)}, u32[]{:S(2)}) collective-permute-start(bf16[384,256]{0,1:T(8,128)(2,1)S(1)} %bitcast.264), channel_id=1, source_target_pairs={{4,0},{8,4},{12,8},{16,12},{20,16},{24,20},{28,24},{32,28},{36,32}... | collective-permute-start | bytes 589832 | tf_op jit(solution)/shard_map/ppermute | solution.py:15
  41.3 28.5 %collective-permute-start.5 = (bf16[384,256]{0,1:T(8,128)(2,1)S(1)}, bf16[384,256]{0,1:T(8,128)(2,1)S(1)}, u32[]{:S(2)}, u32[]{:S(2)}) collective-permute-start(bf16[384,256]{0,1:T(8,128)(2,1)S(1)} %bitcast.274), channel_id=1, source_target_pairs={{4,0},{8,4},{12,8},{16,12},{20,16},{24,20},{28,24},{32,28},{36,32}... | collective-permute-start | bytes 589832 | tf_op jit(solution)/shard_map/ppermute | solution.py:15
  42.6 9.6 %collective-permute-start.18 = (s32[384]{0:T(512)S(1)}, s32[384]{0:T(512)S(1)}, u32[]{:S(2)}, u32[]{:S(2)}) collective-permute-start(s32[384]{0:T(512)S(1)} %collective-permute-done.12), channel_id=1, source_target_pairs={{0,4},{4,8},{8,12},{12,16},{16,20},{20,24},{24,28},{28,32},{32,36}... | collective-permute-start | bytes 4616 | tf_op jit(solution)/shard_map/ppermute | solution.py:15
  50.9 9.0 %collective-permute-start.21 = (s32[384]{0:T(512)S(1)}, s32[384]{0:T(512)S(1)}, u32[]{:S(2)}, u32[]{:S(2)}) collective-permute-start(s32[384]{0:T(512)S(1)} %collective-permute-done.15), channel_id=1, source_target_pairs={{4,0},{8,4},{12,8},{16,12},{20,16},{24,20},{28,24},{32,28},{36,32}... | collective-permute-start | bytes 4616 | tf_op jit(solution)/shard_map/ppermute | solution.py:15
  52.3 19.4 %collective-permute-start.2 = (bf16[384,256]{0,1:T(8,128)(2,1)S(1)}, bf16[384,256]{0,1:T(8,128)(2,1)S(1)}, u32[]{:S(2)}, u32[]{:S(2)}) collective-permute-start(bf16[384,256]{0,1:T(8,128)(2,1)S(1)} %bitcast.275), channel_id=1, source_target_pairs={{0,4},{4,8},{8,12},{12,16},{16,20},{20,24},{24,28},{28,32},{32,36}... | collective-permute-start | bytes 589832 | tf_op jit(solution)/shard_map/ppermute | solution.py:15
  61.5 19.0 %collective-permute-start.7 = (bf16[384,256]{0,1:T(8,128)(2,1)S(1)}, bf16[384,256]{0,1:T(8,128)(2,1)S(1)}, u32[]{:S(2)}, u32[]{:S(2)}) collective-permute-start(bf16[384,256]{0,1:T(8,128)(2,1)S(1)} %collective-permute-done.1), channel_id=1, source_target_pairs={{0,4},{4,8},{8,12},{12,16},{16,20},{20,24},{24,28},{28,32},{32,36}... | collective-permute-start | bytes 589832 | tf_op jit(solution)/shard_map/ppermute | solution.py:15
  68.5 19.0 %collective-permute-start.10 = (bf16[384,256]{0,1:T(8,128)(2,1)S(1)}, bf16[384,256]{0,1:T(8,128)(2,1)S(1)}, u32[]{:S(2)}, u32[]{:S(2)}) collective-permute-start(bf16[384,256]{0,1:T(8,128)(2,1)S(1)} %collective-permute-done.4), channel_id=1, source_target_pairs={{4,0},{8,4},{12,8},{16,12},{20,16},{24,20},{28,24},{32,28},{36,32}... | collective-permute-start | bytes 589832 | tf_op jit(solution)/shard_map/ppermute | solution.py:15
  69.8 19.6 %collective-permute-start.11 = (bf16[384,256]{0,1:T(8,128)(2,1)S(1)}, bf16[384,256]{0,1:T(8,128)(2,1)S(1)}, u32[]{:S(2)}, u32[]{:S(2)}) collective-permute-start(bf16[384,256]{0,1:T(8,128)(2,1)S(1)} %collective-permute-done.5), channel_id=1, source_target_pairs={{4,0},{8,4},{12,8},{16,12},{20,16},{24,20},{28,24},{32,28},{36,32}... | collective-permute-start | bytes 589832 | tf_op jit(solution)/shard_map/ppermute | solution.py:15
  71.7 19.6 %collective-permute-start.8 = (bf16[384,256]{0,1:T(8,128)(2,1)S(1)}, bf16[384,256]{0,1:T(8,128)(2,1)S(1)}, u32[]{:S(2)}, u32[]{:S(2)}) collective-permute-start(bf16[384,256]{0,1:T(8,128)(2,1)S(1)} %collective-permute-done.2), channel_id=1, source_target_pairs={{0,4},{4,8},{8,12},{12,16},{16,20},{20,24},{24,28},{28,32},{32,36}... | collective-permute-start | bytes 589832 | tf_op jit(solution)/shard_map/ppermute | solution.py:15
  80.6 15.4 %collective-permute-start.13 = (bf16[384,256]{0,1:T(8,128)(2,1)S(1)}, bf16[384,256]{0,1:T(8,128)(2,1)S(1)}, u32[]{:S(2)}, u32[]{:S(2)}) collective-permute-start(bf16[384,256]{0,1:T(8,128)(2,1)S(1)} %collective-permute-done.7), channel_id=1, source_target_pairs={{0,4},{4,8},{8,12},{12,16},{16,20},{20,24},{24,28},{28,32},{32,36}... | collective-permute-start | bytes 589832 | tf_op jit(solution)/shard_map/ppermute | solution.py:15
  87.5 15.4 %collective-permute-start.16 = (bf16[384,256]{0,1:T(8,128)(2,1)S(1)}, bf16[384,256]{0,1:T(8,128)(2,1)S(1)}, u32[]{:S(2)}, u32[]{:S(2)}) collective-permute-start(bf16[384,256]{0,1:T(8,128)(2,1)S(1)} %collective-permute-done.10), channel_id=1, source_target_pairs={{4,0},{8,4},{12,8},{16,12},{20,16},{24,20},{28,24},{32,28},{36,32}... | collective-permute-start | bytes 589832 | tf_op jit(solution)/shard_map/ppermute | solution.py:15
  89.4 14.9 %collective-permute-start.17 = (bf16[384,256]{0,1:T(8,128)(2,1)S(1)}, bf16[384,256]{0,1:T(8,128)(2,1)S(1)}, u32[]{:S(2)}, u32[]{:S(2)}) collective-permute-start(bf16[384,256]{0,1:T(8,128)(2,1)S(1)} %collective-permute-done.11), channel_id=1, source_target_pairs={{4,0},{8,4},{12,8},{16,12},{20,16},{24,20},{28,24},{32,28},{36,32}... | collective-permute-start | bytes 589832 | tf_op jit(solution)/shard_map/ppermute | solution.py:15
  91.3 14.9 %collective-permute-start.14 = (bf16[384,256]{0,1:T(8,128)(2,1)S(1)}, bf16[384,256]{0,1:T(8,128)(2,1)S(1)}, u32[]{:S(2)}, u32[]{:S(2)}) collective-permute-start(bf16[384,256]{0,1:T(8,128)(2,1)S(1)} %collective-permute-done.8), channel_id=1, source_target_pairs={{0,4},{4,8},{8,12},{12,16},{16,20},{20,24},{24,28},{28,32},{32,36}... | collective-permute-start | bytes 589832 | tf_op jit(solution)/shard_map/ppermute | solution.py:15
  96.0 15.6 %collective-permute-start.19 = (bf16[384,256]{0,1:T(8,128)(2,1)S(1)}, bf16[384,256]{0,1:T(8,128)(2,1)S(1)}, u32[]{:S(2)}, u32[]{:S(2)}) collective-permute-start(bf16[384,256]{0,1:T(8,128)(2,1)S(1)} %collective-permute-done.13), channel_id=1, source_target_pairs={{0,4},{4,8},{8,12},{12,16},{16,20},{20,24},{24,28},{28,32},{32,36}... | collective-permute-start | bytes 589832 | tf_op jit(solution)/shard_map/ppermute | solution.py:15
  103.0 9.2 %collective-permute-start.22 = (bf16[384,256]{0,1:T(8,128)(2,1)S(1)}, bf16[384,256]{0,1:T(8,128)(2,1)S(1)}, u32[]{:S(2)}, u32[]{:S(2)}) collective-permute-start(bf16[384,256]{0,1:T(8,128)(2,1)S(1)} %collective-permute-done.16), channel_id=1, source_target_pairs={{4,0},{8,4},{12,8},{16,12},{20,16},{24,20},{28,24},{32,28},{36,32}... | collective-permute-start | bytes 589832 | tf_op jit(solution)/shard_map/ppermute | solution.py:15
  104.3 18.0 %collective-permute-start.23 = (bf16[384,256]{0,1:T(8,128)(2,1)S(1)}, bf16[384,256]{0,1:T(8,128)(2,1)S(1)}, u32[]{:S(2)}, u32[]{:S(2)}) collective-permute-start(bf16[384,256]{0,1:T(8,128)(2,1)S(1)} %collective-permute-done.17), channel_id=1, source_target_pairs={{4,0},{8,4},{12,8},{16,12},{20,16},{24,20},{28,24},{32,28},{36,32}... | collective-permute-start | bytes 589832 | tf_op jit(solution)/shard_map/ppermute | solution.py:15
  106.2 16.8 %collective-permute-start.20 = (bf16[384,256]{0,1:T(8,128)(2,1)S(1)}, bf16[384,256]{0,1:T(8,128)(2,1)S(1)}, u32[]{:S(2)}, u32[]{:S(2)}) collective-permute-start(bf16[384,256]{0,1:T(8,128)(2,1)S(1)} %collective-permute-done.14), channel_id=1, source_target_pairs={{0,4},{4,8},{8,12},{12,16},{16,20},{20,24},{24,28},{28,32},{32,36}... | collective-permute-start | bytes 589832 | tf_op jit(solution)/shard_map/ppermute | solution.py:15
  123.0 1.0 copy-start.1
  124.0 79.7 %copy-start.2 = (f32[1024]{0:T(1024)S(1)}, f32[1024]{0:T(1024)}, u32[]{:S(2)}) copy-start(f32[1024]{0:T(1024)} %param.13) | copy-start | bytes 12292
  125.3 109.1 %reduce-scatter.2.cloned.1.call-start = ((), (), s32[]{:S(2)}) async-start(), calls=%async_computation.2 | async-start | bytes 983040 | tf_op jit(solution)/shard_map/reduce_scatter | solution.py:81
Sparse Core Ops, SparseCore 0:
  125.4 75.7 all-reduce.1
  211.5 22.8 reduce-scatter.1
where the time goes:
time: 244 us; the launch traced here: 243 us
  waiting for transfers between devices  99 us (41%)
  starting transfers between devices  86.3 us (35%)
  matrix products  22.9 us (9%)
  between operations  13.9 us (6%)
  other arithmetic  11.2 us (5%)
  blocking collectives  9.6 us (4%)
    ppermute x24, starting transfers between devices, shifted(): return lax.ppermute(block, axis, route)  86.2 us
    psum x1, waiting for transfers between devices, shards(): lax.psum(attn_part.astype(jnp.bfloat16), 'tp').astype(jnp.float32)  75.8 us
    reduce_scatter x1, waiting for transfers between devices, shards(): lax.psum_scatter(ffn_part.astype(jnp.bfloat16), 'tp', scatter_dimension=1...  23.1 us
    all_gather x1, blocking collectives, shards(): lax.all_gather(hit_features, 'tp', axis=1, tiled=True).astype(jnp.float32)  9.6 us
    dot_general x1, matrix products, shards(): ffn_part = jnp.dot(hidden, w_down, preferred_element_type=jnp.float32)  7.62 us
    dot_general x9, matrix products, absorb(): jnp.einsum('hqk,khd->hqd', powered.astype(jnp.bfloat16), value_heads, pre...  6.29 us
    dot_general x9, matrix products, absorb(): jnp.einsum('qhd,khd->hqk', query_heads, key_heads, preferred_element_type...  5.23 us
  transfers between devices with their start and end apart: 26, of which 2 were waited for; matrix products, arithmetic and copies ran while one was open for 8% of the time, Pallas kernels for 0%

commit v1 on v0

--- a/solution.py
+++ b/solution.py
@@ -7,6 +7,11 @@
 REACH = 4
 epsilon = 1e-05
 neg_fill = -1e30
+
+
+def exchange_gather(shard, axis, dim):
+    repeated = jnp.stack([shard] * lax.axis_size(axis))
+    return jnp.concatenate(lax.all_to_all(repeated, axis, 0, 0), axis=dim)
 
 
 def shifted(block, axis, distance):
@@ -42,7 +47,7 @@
 
 
 def shards(hit_features, segment, norm1_gain, w_qkv, w_out, norm2_gain, w_up, w_down):
-    features = lax.all_gather(hit_features, "tp", axis=1, tiled=True).astype(jnp.float32)
+    features = exchange_gather(hit_features, "tp", 1).astype(jnp.float32)
     normed = rms_scale(features, norm1_gain).astype(jnp.bfloat16)
     projected = jnp.einsum("td,cde->cte", normed, w_qkv, preferred_element_type=jnp.float32)
     queries = (projected[0] * HEAD_DIM ** (-0.5)).astype(jnp.bfloat16)

time: 244 us -> 252 us (1.033)
  blocking collectives: 9.6 us -> 0 us
  waiting for transfers between devices: 99 us -> 107 us
  starting transfers between devices: 86.3 us -> 92.6 us
  local copies, waits for them, and re-layouts: 0.2 us -> 3.95 us
    all_gather x1 -> x0, blocking collectives: 9.6 us -> none  [shards(): lax.all_gather(hit_features, 'tp', axis=1, tiled=True).astype(jnp.float32)]
    ppermute x24, waiting for transfers between devices: 0.06 us -> 7.09 us  [shifted(): return lax.ppermute(block, axis, route)]
    all_to_all x0 -> x1, starting transfers between devices: none -> 6.66 us  [exchange_gather(): return jnp.concatenate(lax.all_to_all(repeated, axis, 0, 0), axis=dim)]
    reduce_sum x1 -> x2, other arithmetic: 0.23 us -> 3.19 us  [rms_scale(): mean_square = jnp.mean(features * features, axis=-1, keepdims=True)]
    add x1 -> x0, other arithmetic: 2.53 us -> none  [shards(): features + lax.psum(attn_part.astype(jnp.bfloat16), 'tp').astype(jnp.floa...]
  transfers between devices with their start and end apart: 26 -> 27, of which waited for: 2 -> 3; matrix products, arithmetic and copies ran while one was open for 8% -> 7% of each run, Pallas kernels for 0% -> 0%
where the time goes in v1:
time: 252 us; the launch traced here: 251 us
  waiting for transfers between devices  107 us (42%)
  starting transfers between devices  92.6 us (37%)
  matrix products  21.7 us (9%)
  between operations  14.1 us (6%)
  other arithmetic  11.8 us (5%)
  local copies, waits for them, and re-layouts  3.95 us (2%)
    ppermute x24, starting transfers between devices, shifted(): return lax.ppermute(block, axis, route)  85.9 us
    psum x1, waiting for transfers between devices, shards(): lax.psum(attn_part.astype(jnp.bfloat16), 'tp').astype(jnp.float32)  77.3 us
    reduce_scatter x1, waiting for transfers between devices, shards(): lax.psum_scatter(ffn_part.astype(jnp.bfloat16), 'tp', scatter_dimension=1...  23.1 us
    dot_general x1, matrix products, shards(): ffn_part = jnp.dot(hidden, w_down, preferred_element_type=jnp.float32)  7.82 us
    ppermute x24, waiting for transfers between devices, shifted(): return lax.ppermute(block, axis, route)  7.09 us
    all_to_all x1, starting transfers between devices, exchange_gather(): return jnp.concatenate(lax.all_to_all(repeated, axis, 0, 0), axis=dim)  6.66 us
    dot_general x9, matrix products, absorb(): jnp.einsum('hqk,khd->hqd', powered.astype(jnp.bfloat16), value_heads, pre...  6.26 us
    dot_general x9, matrix products, absorb(): jnp.einsum('qhd,khd->hqk', query_heads, key_heads, preferred_element_type...  5.2 us
  transfers between devices with their start and end apart: 27, of which 3 were waited for; matrix products, arithmetic and copies ran while one was open for 7% of the time, Pallas kernels for 0%

profile of v1, /device:TPU:1, one launch (start us, length us, event | category | flops | bytes accessed | tf_op | source)
XLA Modules:
  0.0 251.4 jit_solution(17344244168852457251)
XLA Ops:
  6.5 2.0 stack.2
  8.6 6.7 %all-to-all-start = ((bf16[4,384,256]{2,1,0:T(8,128)(2,1)}), bf16[4,384,256]{2,1,0:T(8,128)(2,1)S(1)}, u32[]{:S(2)}, u32[]{:S(2)}) async-start(bf16[4,384,256]{2,1,0:T(8,128)(2,1)} %stack.2), calls=%async_computation | async-start | bytes 1572864 | tf_op jit(solution)/shard_map/all_to_all | solution.py:14
  15.2 1.5 collective-permute-start
  16.7 1.3 collective-permute-start.3
  18.0 4.0 %collective-permute-start.6 = (s32[384]{0:T(512)S(1)}, s32[384]{0:T(512)S(1)}, u32[]{:S(2)}, u32[]{:S(2)}) collective-permute-start(s32[384]{0:T(512)S(1)} %collective-permute-done), channel_id=1, source_target_pairs={{0,4},{4,8},{8,12},{12,16},{16,20},{20,24},{24,28},{28,32},{32,36}... | collective-permute-start | bytes 4616 | tf_op jit(solution)/shard_map/ppermute | solution.py:20
  22.0 1.3 collective-permute-start.9
  23.4 4.0 %collective-permute-start.12 = (s32[384]{0:T(512)S(1)}, s32[384]{0:T(512)S(1)}, u32[]{:S(2)}, u32[]{:S(2)}) collective-permute-start(s32[384]{0:T(512)S(1)} %collective-permute-done.6), channel_id=1, source_target_pairs={{0,4},{4,8},{8,12},{12,16},{16,20},{20,24},{24,28},{28,32},{32,36}... | collective-permute-start | bytes 4616 | tf_op jit(solution)/shard_map/ppermute | solution.py:20
  27.4 1.3 collective-permute-start.15
  28.7 7.1 %collective-permute-start.18 = (s32[384]{0:T(512)S(1)}, s32[384]{0:T(512)S(1)}, u32[]{:S(2)}, u32[]{:S(2)}) collective-permute-start(s32[384]{0:T(512)S(1)} %collective-permute-done.12), channel_id=1, source_target_pairs={{0,4},{4,8},{8,12},{12,16},{16,20},{20,24},{24,28},{28,32},{32,36}... | collective-permute-start | bytes 4616 | tf_op jit(solution)/shard_map/ppermute | solution.py:20
  35.8 1.3 collective-permute-start.21
  37.1 7.0 %collective-permute-done.21 = s32[384]{0:T(512)S(1)} collective-permute-done((s32[384]{0:T(512)S(1)}, s32[384]{0:T(512)S(1)}, u32[]{:S(2)}, u32[]{:S(2)}) %collective-permute-start.21) | collective-permute-done | bytes 1568 | tf_op jit(solution)/shard_map/ppermute | solution.py:20
  44.1 1.9 broadcast_compare_fusion.8
  46.6 1.5 copy-done.2
  48.1 1.1 convolution_bitcast_fusion
  49.3 7.0 %collective-permute-start.1 = (bf16[384,256]{0,1:T(8,128)(2,1)S(1)}, bf16[384,256]{0,1:T(8,128)(2,1)S(1)}, u32[]{:S(2)}, u32[]{:S(2)}) collective-permute-start(bf16[384,256]{0,1:T(8,128)(2,1)S(1)} %bitcast.269), channel_id=1, source_target_pairs={{0,4},{4,8},{8,12},{12,16},{16,20},{20,24},{24,28},{28,32},{32,36}... | collective-permute-start | bytes 589832 | tf_op jit(solution)/shard_map/ppermute | solution.py:20
  56.3 1.3 collective-permute-start.4
  57.6 1.3 collective-permute-start.5
  58.9 8.2 %collective-permute-start.2 = (bf16[384,256]{0,1:T(8,128)(2,1)S(1)}, bf16[384,256]{0,1:T(8,128)(2,1)S(1)}, u32[]{:S(2)}, u32[]{:S(2)}) collective-permute-start(bf16[384,256]{0,1:T(8,128)(2,1)S(1)} %bitcast.281), channel_id=1, source_target_pairs={{0,4},{4,8},{8,12},{12,16},{16,20},{20,24},{24,28},{28,32},{32,36}... | collective-permute-start | bytes 589832 | tf_op jit(solution)/shard_map/ppermute | solution.py:20
  67.8 7.0 %collective-permute-start.7 = (bf16[384,256]{0,1:T(8,128)(2,1)S(1)}, bf16[384,256]{0,1:T(8,128)(2,1)S(1)}, u32[]{:S(2)}, u32[]{:S(2)}) collective-permute-start(bf16[384,256]{0,1:T(8,128)(2,1)S(1)} %collective-permute-done.1), channel_id=1, source_target_pairs={{0,4},{4,8},{8,12},{12,16},{16,20},{20,24},{24,28},{28,32},{32,36}... | collective-permute-start | bytes 589832 | tf_op jit(solution)/shard_map/ppermute | solution.py:20
  74.8 1.3 collective-permute-start.10
  76.1 1.3 collective-permute-start.11
  78.0 4.6 %collective-permute-start.8 = (bf16[384,256]{0,1:T(8,128)(2,1)S(1)}, bf16[384,256]{0,1:T(8,128)(2,1)S(1)}, u32[]{:S(2)}, u32[]{:S(2)}) collective-permute-start(bf16[384,256]{0,1:T(8,128)(2,1)S(1)} %collective-permute-done.2), channel_id=1, source_target_pairs={{0,4},{4,8},{8,12},{12,16},{16,20},{20,24},{24,28},{28,32},{32,36}... | collective-permute-start | bytes 589832 | tf_op jit(solution)/shard_map/ppermute | solution.py:20
  83.2 1.3 collective-permute-start.16
  84.6 7.6 %collective-permute-start.13 = (bf16[384,256]{0,1:T(8,128)(2,1)S(1)}, bf16[384,256]{0,1:T(8,128)(2,1)S(1)}, u32[]{:S(2)}, u32[]{:S(2)}) collective-permute-start(bf16[384,256]{0,1:T(8,128)(2,1)S(1)} %collective-permute-done.7), channel_id=1, source_target_pairs={{0,4},{4,8},{8,12},{12,16},{16,20},{20,24},{24,28},{28,32},{32,36}... | collective-permute-start | bytes 589832 | tf_op jit(solution)/shard_map/ppermute | solution.py:20
  92.8 1.3 collective-permute-start.17
  94.7 4.0 %collective-permute-start.14 = (bf16[384,256]{0,1:T(8,128)(2,1)S(1)}, bf16[384,256]{0,1:T(8,128)(2,1)S(1)}, u32[]{:S(2)}, u32[]{:S(2)}) collective-permute-start(bf16[384,256]{0,1:T(8,128)(2,1)S(1)} %collective-permute-done.8), channel_id=1, source_target_pairs={{0,4},{4,8},{8,12},{12,16},{16,20},{20,24},{24,28},{28,32},{32,36}... | collective-permute-start | bytes 589832 | tf_op jit(solution)/shard_map/ppermute | solution.py:20
  98.7 7.0 %collective-permute-start.19 = (bf16[384,256]{0,1:T(8,128)(2,1)S(1)}, bf16[384,256]{0,1:T(8,128)(2,1)S(1)}, u32[]{:S(2)}, u32[]{:S(2)}) collective-permute-start(bf16[384,256]{0,1:T(8,128)(2,1)S(1)} %collective-permute-done.13), channel_id=1, source_target_pairs={{0,4},{4,8},{8,12},{12,16},{16,20},{20,24},{24,28},{28,32},{32,36}... | collective-permute-start | bytes 589832 | tf_op jit(solution)/shard_map/ppermute | solution.py:20
  105.7 1.3 collective-permute-start.22
  107.0 1.3 collective-permute-start.23
  108.9 8.4 %collective-permute-start.20 = (bf16[384,256]{0,1:T(8,128)(2,1)S(1)}, bf16[384,256]{0,1:T(8,128)(2,1)S(1)}, u32[]{:S(2)}, u32[]{:S(2)}) collective-permute-start(bf16[384,256]{0,1:T(8,128)(2,1)S(1)} %collective-permute-done.14), channel_id=1, source_target_pairs={{0,4},{4,8},{8,12},{12,16},{16,20},{20,24},{24,28},{28,32},{32,36}... | collective-permute-start | bytes 589832 | tf_op jit(solution)/shard_map/ppermute | solution.py:20
  119.1 0.7 convolution_bitcast_fusion.7
  119.8 1.0 fusion.4
  121.5 1.0 fusion.8
  122.5 0.7 convolution_bitcast_fusion.3
  123.2 1.0 fusion.12
  124.7 1.0 fusion
  125.8 0.7 fusion.34
  126.5 0.7 fusion.37
  127.1 0.7 fusion.40
  127.8 0.7 fusion.43
  128.6 0.7 convolution_bitcast_fusion.1
  129.2 0.9 fusion.83
  130.3 1.3 convolution_convert_fusion
  131.6 77.3 %all-reduce.2.cloned.1.call-done = bf16[384,1024]{1,0:T(8,128)(2,1)} async-done(((bf16[384,1024]{1,0:T(8,128)(2,1)}), bf16[384,1024]{1,0:T(8,128)(2,1)}) %all-reduce.2.cloned.1.call-update) | async-done | bytes 786448 | tf_op jit(solution)/shard_map/psum | solution.py:80
  208.9 3.0 %multiply_reduce_fusion = (f32[384]{0:T(512)S(1)}, f32[384,1024]{1,0:T(8,128)}) fusion(f32[384,1024]{1,0:T(8,128)} %bitcast.268, bf16[384,1024]{1,0:T(8,128)(2,1)} %all-reduce.2.cloned.1.call-done), kind=kLoop, calls=%fused_computation.57 | loop fusion | flops 1572480 | bytes 3933696 | tf_op jit(solution)/shard_map/reduce_sum | solution.py:24
  211.9 7.8 %convolution_convert_fusion.1 = bf16[384,1024]{1,0:T(8,128)(2,1)} fusion(bf16[1024,1024]{1,0:T(8,128)(2,1)S(1)} %copy-done, bf16[1024,1024]{1,0:T(8,128)(2,1)} %param.14, f32[384,1024]{1,0:T(8,128)} %get-tuple-element.6, f32[1024]{0:T(1024)S(1)} %copy-done.11, f32[384]{0:T(512)S(1)} %add_rsqrt_fusion), kind=kOutput, calls=%fused_computation.64 | convolution fusion | flops 1637744640 | bytes 6559232 | tf_op jit(solution)/shard_map/dot_general | solution.py:85
  219.7 23.1 %reduce-scatter.2.cloned.1.call-done = bf16[384,256]{1,0:T(8,128)(2,1)} async-done(((bf16[384,1024]{1,0:T(8,128)(2,1)}), bf16[384,256]{1,0:T(8,128)(2,1)}) %reduce-scatter.2.cloned.1.call-update) | async-done | bytes 196624 | tf_op jit(solution)/shard_map/reduce_scatter | solution.py:86
  242.8 1.8 add_convert_fusion
  (73 shorter events, 7.4 us)
Async XLA Ops:
  6.5 205.3 %copy-start = (bf16[1024,1024]{1,0:T(8,128)(2,1)S(1)}, bf16[1024,1024]{1,0:T(8,128)(2,1)}, u32[]{:S(2)}) copy-start(bf16[1024,1024]{1,0:T(8,128)(2,1)} %param.15) | copy-start | bytes 6291460
  6.5 8.7 %copy-start.10 = (s32[384]{0:T(512)S(1)}, s32[384]{0:T(512)}, u32[]{:S(2)}) copy-start(s32[384]{0:T(512)} %param.9) | copy-start | bytes 4612
  8.6 37.5 %all-to-all-start = ((bf16[4,384,256]{2,1,0:T(8,128)(2,1)}), bf16[4,384,256]{2,1,0:T(8,128)(2,1)S(1)}, u32[]{:S(2)}, u32[]{:S(2)}) async-start(bf16[4,384,256]{2,1,0:T(8,128)(2,1)} %stack.2), calls=%async_computation | async-start | bytes 1572864 | tf_op jit(solution)/shard_map/all_to_all | solution.py:14
  15.2 193.7 %all-reduce.2.cloned.1.call-start = ((), (), s32[]{:S(2)}) async-start(), calls=%async_computation.2 | async-start | bytes 1572864 | tf_op jit(solution)/shard_map/psum | solution.py:80
  15.2 2.8 %collective-permute-start = (s32[384]{0:T(512)S(1)}, s32[384]{0:T(512)S(1)}, u32[]{:S(2)}, u32[]{:S(2)}) collective-permute-start(s32[384]{0:T(512)S(1)} %broadcast_add_fusion), channel_id=1, source_target_pairs={{0,4},{4,8},{8,12},{12,16},{16,20},{20,24},{24,28},{28,32},{32,36}... | collective-permute-start | bytes 4616 | tf_op jit(solution)/shard_map/ppermute | solution.py:20
  16.7 5.3 %collective-permute-start.3 = (s32[384]{0:T(512)S(1)}, s32[384]{0:T(512)S(1)}, u32[]{:S(2)}, u32[]{:S(2)}) collective-permute-start(s32[384]{0:T(512)S(1)} %broadcast_add_fusion), channel_id=1, source_target_pairs={{4,0},{8,4},{12,8},{16,12},{20,16},{24,20},{28,24},{32,28},{36,32}... | collective-permute-start | bytes 4616 | tf_op jit(solution)/shard_map/ppermute | solution.py:20
  18.0 5.3 %collective-permute-start.6 = (s32[384]{0:T(512)S(1)}, s32[384]{0:T(512)S(1)}, u32[]{:S(2)}, u32[]{:S(2)}) collective-permute-start(s32[384]{0:T(512)S(1)} %collective-permute-done), channel_id=1, source_target_pairs={{0,4},{4,8},{8,12},{12,16},{16,20},{20,24},{24,28},{28,32},{32,36}... | collective-permute-start | bytes 4616 | tf_op jit(solution)/shard_map/ppermute | solution.py:20
  22.0 5.3 %collective-permute-start.9 = (s32[384]{0:T(512)S(1)}, s32[384]{0:T(512)S(1)}, u32[]{:S(2)}, u32[]{:S(2)}) collective-permute-start(s32[384]{0:T(512)S(1)} %collective-permute-done.3), channel_id=1, source_target_pairs={{4,0},{8,4},{12,8},{16,12},{20,16},{24,20},{28,24},{32,28},{36,32}... | collective-permute-start | bytes 4616 | tf_op jit(solution)/shard_map/ppermute | solution.py:20
  23.4 5.3 %collective-permute-start.12 = (s32[384]{0:T(512)S(1)}, s32[384]{0:T(512)S(1)}, u32[]{:S(2)}, u32[]{:S(2)}) collective-permute-start(s32[384]{0:T(512)S(1)} %collective-permute-done.6), channel_id=1, source_target_pairs={{0,4},{4,8},{8,12},{12,16},{16,20},{20,24},{24,28},{28,32},{32,36}... | collective-permute-start | bytes 4616 | tf_op jit(solution)/shard_map/ppermute | solution.py:20
  27.4 8.4 %collective-permute-start.15 = (s32[384]{0:T(512)S(1)}, s32[384]{0:T(512)S(1)}, u32[]{:S(2)}, u32[]{:S(2)}) collective-permute-start(s32[384]{0:T(512)S(1)} %collective-permute-done.9), channel_id=1, source_target_pairs={{4,0},{8,4},{12,8},{16,12},{20,16},{24,20},{28,24},{32,28},{36,32}... | collective-permute-start | bytes 4616 | tf_op jit(solution)/shard_map/ppermute | solution.py:20
  28.7 8.4 %collective-permute-start.18 = (s32[384]{0:T(512)S(1)}, s32[384]{0:T(512)S(1)}, u32[]{:S(2)}, u32[]{:S(2)}) collective-permute-start(s32[384]{0:T(512)S(1)} %collective-permute-done.12), channel_id=1, source_target_pairs={{0,4},{4,8},{8,12},{12,16},{16,20},{20,24},{24,28},{28,32},{32,36}... | collective-permute-start | bytes 4616 | tf_op jit(solution)/shard_map/ppermute | solution.py:20
  35.8 8.3 %collective-permute-start.21 = (s32[384]{0:T(512)S(1)}, s32[384]{0:T(512)S(1)}, u32[]{:S(2)}, u32[]{:S(2)}) collective-permute-start(s32[384]{0:T(512)S(1)} %collective-permute-done.15), channel_id=1, source_target_pairs={{4,0},{8,4},{12,8},{16,12},{20,16},{24,20},{28,24},{32,28},{36,32}... | collective-permute-start | bytes 4616 | tf_op jit(solution)/shard_map/ppermute | solution.py:20
  46.1 2.0 copy-start.2
  46.2 2.0 copy-start.9
  46.4 2.9 %copy-start.1 = (f32[4,48,8,256]{3,2,0,1:T(8,128)}, f32[4,48,8,256]{3,2,0,1:T(8,128)S(1)}, u32[]{:S(2)}) copy-start(f32[4,48,8,256]{3,2,0,1:T(8,128)S(1)} %copy.40) | copy-start | bytes 4718596
  48.1 19.1 %copy-start.4 = (pred[384,384]{0,1:T(8,128)(4,1)S(1)}, pred[384,384]{0,1:T(8,128)(4,1)}, u32[]{:S(2)}) copy-start(pred[384,384]{0,1:T(8,128)(4,1)} %get-tuple-element.30) | copy-start | bytes 442372
  49.2 28.2 %copy-start.3 = (pred[384,384]{0,1:T(8,128)(4,1)S(1)}, pred[384,384]{0,1:T(8,128)(4,1)}, u32[]{:S(2)}) copy-start(pred[384,384]{0,1:T(8,128)(4,1)} %get-tuple-element.38) | copy-start | bytes 442372
  49.3 18.4 %collective-permute-start.1 = (bf16[384,256]{0,1:T(8,128)(2,1)S(1)}, bf16[384,256]{0,1:T(8,128)(2,1)S(1)}, u32[]{:S(2)}, u32[]{:S(2)}) collective-permute-start(bf16[384,256]{0,1:T(8,128)(2,1)S(1)} %bitcast.269), channel_id=1, source_target_pairs={{0,4},{4,8},{8,12},{12,16},{16,20},{20,24},{24,28},{28,32},{32,36}... | collective-permute-start | bytes 589832 | tf_op jit(solution)/shard_map/ppermute | solution.py:20
  56.3 18.4 %collective-permute-start.4 = (bf16[384,256]{0,1:T(8,128)(2,1)S(1)}, bf16[384,256]{0,1:T(8,128)(2,1)S(1)}, u32[]{:S(2)}, u32[]{:S(2)}) collective-permute-start(bf16[384,256]{0,1:T(8,128)(2,1)S(1)} %bitcast.270), channel_id=1, source_target_pairs={{4,0},{8,4},{12,8},{16,12},{20,16},{24,20},{28,24},{32,28},{36,32}... | collective-permute-start | bytes 589832 | tf_op jit(solution)/shard_map/ppermute | solution.py:20
  57.6 18.4 %collective-permute-start.5 = (bf16[384,256]{0,1:T(8,128)(2,1)S(1)}, bf16[384,256]{0,1:T(8,128)(2,1)S(1)}, u32[]{:S(2)}, u32[]{:S(2)}) collective-permute-start(bf16[384,256]{0,1:T(8,128)(2,1)S(1)} %bitcast.280), channel_id=1, source_target_pairs={{4,0},{8,4},{12,8},{16,12},{20,16},{24,20},{28,24},{32,28},{36,32}... | collective-permute-start | bytes 589832 | tf_op jit(solution)/shard_map/ppermute | solution.py:20
  58.9 19.0 %collective-permute-start.2 = (bf16[384,256]{0,1:T(8,128)(2,1)S(1)}, bf16[384,256]{0,1:T(8,128)(2,1)S(1)}, u32[]{:S(2)}, u32[]{:S(2)}) collective-permute-start(bf16[384,256]{0,1:T(8,128)(2,1)S(1)} %bitcast.281), channel_id=1, source_target_pairs={{0,4},{4,8},{8,12},{12,16},{16,20},{20,24},{24,28},{28,32},{32,36}... | collective-permute-start | bytes 589832 | tf_op jit(solution)/shard_map/ppermute | solution.py:20
  67.2 15.4 %copy-start.7 = (pred[384,384]{0,1:T(8,128)(4,1)S(1)}, pred[384,384]{0,1:T(8,128)(4,1)}, u32[]{:S(2)}) copy-start(pred[384,384]{0,1:T(8,128)(4,1)} %get-tuple-element.31) | copy-start | bytes 442372
  67.8 16.8 %collective-permute-start.7 = (bf16[384,256]{0,1:T(8,128)(2,1)S(1)}, bf16[384,256]{0,1:T(8,128)(2,1)S(1)}, u32[]{:S(2)}, u32[]{:S(2)}) collective-permute-start(bf16[384,256]{0,1:T(8,128)(2,1)S(1)} %collective-permute-done.1), channel_id=1, source_target_pairs={{0,4},{4,8},{8,12},{12,16},{16,20},{20,24},{24,28},{28,32},{32,36}... | collective-permute-start | bytes 589832 | tf_op jit(solution)/shard_map/ppermute | solution.py:20
  74.8 8.5 %collective-permute-start.10 = (bf16[384,256]{0,1:T(8,128)(2,1)S(1)}, bf16[384,256]{0,1:T(8,128)(2,1)S(1)}, u32[]{:S(2)}, u32[]{:S(2)}) collective-permute-start(bf16[384,256]{0,1:T(8,128)(2,1)S(1)} %collective-permute-done.4), channel_id=1, source_target_pairs={{4,0},{8,4},{12,8},{16,12},{20,16},{24,20},{28,24},{32,28},{36,32}... | collective-permute-start | bytes 589832 | tf_op jit(solution)/shard_map/ppermute | solution.py:20
  76.1 16.7 %collective-permute-start.11 = (bf16[384,256]{0,1:T(8,128)(2,1)S(1)}, bf16[384,256]{0,1:T(8,128)(2,1)S(1)}, u32[]{:S(2)}, u32[]{:S(2)}) collective-permute-start(bf16[384,256]{0,1:T(8,128)(2,1)S(1)} %collective-permute-done.5), channel_id=1, source_target_pairs={{4,0},{8,4},{12,8},{16,12},{20,16},{24,20},{28,24},{32,28},{36,32}... | collective-permute-start | bytes 589832 | tf_op jit(solution)/shard_map/ppermute | solution.py:20
  78.0 16.7 %collective-permute-start.8 = (bf16[384,256]{0,1:T(8,128)(2,1)S(1)}, bf16[384,256]{0,1:T(8,128)(2,1)S(1)}, u32[]{:S(2)}, u32[]{:S(2)}) collective-permute-start(bf16[384,256]{0,1:T(8,128)(2,1)S(1)} %collective-permute-done.2), channel_id=1, source_target_pairs={{0,4},{4,8},{8,12},{12,16},{16,20},{20,24},{24,28},{28,32},{32,36}... | collective-permute-start | bytes 589832 | tf_op jit(solution)/shard_map/ppermute | solution.py:20
  82.6 11.4 %copy-start.6 = (pred[384,384]{0,1:T(8,128)(4,1)S(1)}, pred[384,384]{0,1:T(8,128)(4,1)}, u32[]{:S(2)}) copy-start(pred[384,384]{0,1:T(8,128)(4,1)} %get-tuple-element.33) | copy-start | bytes 442372
  83.2 22.4 %collective-permute-start.16 = (bf16[384,256]{0,1:T(8,128)(2,1)S(1)}, bf16[384,256]{0,1:T(8,128)(2,1)S(1)}, u32[]{:S(2)}, u32[]{:S(2)}) collective-permute-start(bf16[384,256]{0,1:T(8,128)(2,1)S(1)} %collective-permute-done.10), channel_id=1, source_target_pairs={{4,0},{8,4},{12,8},{16,12},{20,16},{24,20},{28,24},{32,28},{36,32}... | collective-permute-start | bytes 589832 | tf_op jit(solution)/shard_map/ppermute | solution.py:20
  84.6 14.1 %collective-permute-start.13 = (bf16[384,256]{0,1:T(8,128)(2,1)S(1)}, bf16[384,256]{0,1:T(8,128)(2,1)S(1)}, u32[]{:S(2)}, u32[]{:S(2)}) collective-permute-start(bf16[384,256]{0,1:T(8,128)(2,1)S(1)} %collective-permute-done.7), channel_id=1, source_target_pairs={{0,4},{4,8},{8,12},{12,16},{16,20},{20,24},{24,28},{28,32},{32,36}... | collective-permute-start | bytes 589832 | tf_op jit(solution)/shard_map/ppermute | solution.py:20
  92.2 16.1 %copy-start.5 = (pred[384,384]{0,1:T(8,128)(4,1)S(1)}, pred[384,384]{0,1:T(8,128)(4,1)}, u32[]{:S(2)}) copy-start(pred[384,384]{0,1:T(8,128)(4,1)} %get-tuple-element.35) | copy-start | bytes 442372
  92.8 14.2 %collective-permute-start.17 = (bf16[384,256]{0,1:T(8,128)(2,1)S(1)}, bf16[384,256]{0,1:T(8,128)(2,1)S(1)}, u32[]{:S(2)}, u32[]{:S(2)}) collective-permute-start(bf16[384,256]{0,1:T(8,128)(2,1)S(1)} %collective-permute-done.11), channel_id=1, source_target_pairs={{4,0},{8,4},{12,8},{16,12},{20,16},{24,20},{28,24},{32,28},{36,32}... | collective-permute-start | bytes 589832 | tf_op jit(solution)/shard_map/ppermute | solution.py:20
  94.7 14.2 %collective-permute-start.14 = (bf16[384,256]{0,1:T(8,128)(2,1)S(1)}, bf16[384,256]{0,1:T(8,128)(2,1)S(1)}, u32[]{:S(2)}, u32[]{:S(2)}) collective-permute-start(bf16[384,256]{0,1:T(8,128)(2,1)S(1)} %collective-permute-done.8), channel_id=1, source_target_pairs={{0,4},{4,8},{8,12},{12,16},{16,20},{20,24},{24,28},{28,32},{32,36}... | collective-permute-start | bytes 589832 | tf_op jit(solution)/shard_map/ppermute | solution.py:20
  98.7 19.2 %collective-permute-start.19 = (bf16[384,256]{0,1:T(8,128)(2,1)S(1)}, bf16[384,256]{0,1:T(8,128)(2,1)S(1)}, u32[]{:S(2)}, u32[]{:S(2)}) collective-permute-start(bf16[384,256]{0,1:T(8,128)(2,1)S(1)} %collective-permute-done.13), channel_id=1, source_target_pairs={{0,4},{4,8},{8,12},{12,16},{16,20},{20,24},{24,28},{28,32},{32,36}... | collective-permute-start | bytes 589832 | tf_op jit(solution)/shard_map/ppermute | solution.py:20
  105.7 12.8 %collective-permute-start.22 = (bf16[384,256]{0,1:T(8,128)(2,1)S(1)}, bf16[384,256]{0,1:T(8,128)(2,1)S(1)}, u32[]{:S(2)}, u32[]{:S(2)}) collective-permute-start(bf16[384,256]{0,1:T(8,128)(2,1)S(1)} %collective-permute-done.16), channel_id=1, source_target_pairs={{4,0},{8,4},{12,8},{16,12},{20,16},{24,20},{28,24},{32,28},{36,32}... | collective-permute-start | bytes 589832 | tf_op jit(solution)/shard_map/ppermute | solution.py:20
  107.0 21.5 %collective-permute-start.23 = (bf16[384,256]{0,1:T(8,128)(2,1)S(1)}, bf16[384,256]{0,1:T(8,128)(2,1)S(1)}, u32[]{:S(2)}, u32[]{:S(2)}) collective-permute-start(bf16[384,256]{0,1:T(8,128)(2,1)S(1)} %collective-permute-done.17), channel_id=1, source_target_pairs={{4,0},{8,4},{12,8},{16,12},{20,16},{24,20},{28,24},{32,28},{36,32}... | collective-permute-start | bytes 589832 | tf_op jit(solution)/shard_map/ppermute | solution.py:20
  108.9 20.3 %collective-permute-start.20 = (bf16[384,256]{0,1:T(8,128)(2,1)S(1)}, bf16[384,256]{0,1:T(8,128)(2,1)S(1)}, u32[]{:S(2)}, u32[]{:S(2)}) collective-permute-start(bf16[384,256]{0,1:T(8,128)(2,1)S(1)} %collective-permute-done.14), channel_id=1, source_target_pairs={{0,4},{4,8},{8,12},{12,16},{16,20},{20,24},{24,28},{28,32},{32,36}... | collective-permute-start | bytes 589832 | tf_op jit(solution)/shard_map/ppermute | solution.py:20
  129.2 1.0 copy-start.8
  131.6 80.3 %copy-start.11 = (f32[1024]{0:T(1024)S(1)}, f32[1024]{0:T(1024)}, u32[]{:S(2)}) copy-start(f32[1024]{0:T(1024)} %param.13) | copy-start | bytes 12292
  131.6 111.2 %reduce-scatter.2.cloned.1.call-start = ((), (), s32[]{:S(2)}) async-start(), calls=%async_computation.3 | async-start | bytes 983040 | tf_op jit(solution)/shard_map/reduce_scatter | solution.py:86
Sparse Core Ops, SparseCore 0:
  131.7 77.1 all-reduce.1
  219.8 22.8 reduce-scatter.1
